TPU v7x, 32 devices: a whole 2x2x4 slice. The times are simulated.
32 devices in a mesh: expert: 2 (over x), seq: 4 (over z), fsdp: 4 (over y, core).
Axes of the slice: x: 2, y: 2, z: 4, core: 2. Of those that a mesh axis runs over, the one named last changes fastest.
Arguments:
- queries: bfloat16 [16384, 5120], P(('expert', 'seq', 'fsdp')), parts along dimension 0, may hold values from -100 to 100
- keys: bfloat16 [16384, 5120], P(('expert', 'seq', 'fsdp')), parts along dimension 0, may hold values from -100 to 100
- values: bfloat16 [16384, 5120], P(('expert', 'seq', 'fsdp')), parts along dimension 0, may hold values from -6 to 6
- query_gain: float32 [10240], P('expert'), parts along dimension 0, may hold values from 1 to 3
- key_gain: float32 [10240], P('expert'), parts along dimension 0, may hold values from 1 to 3
- timestep: int32 [2], P('expert'), parts along dimension 0, may hold values from 0 to 999, as said below
- gate_base: float32 [10240], P('expert'), parts along dimension 0, may hold values from -3 to 3
- time_weight: float32 [512, 5120], P('expert'), parts along dimension 0, may hold values from -0.375 to 0.375
Outputs:
- attended: bfloat16 [16384, 5120], P(('expert', 'seq', 'fsdp')), parts along dimension 0
There are 2 independent parts, one for each index of `expert`. A program takes and returns all parts, laid end to end along the dimension named above; each array names one. Nothing has to cross between parts.
Inputs may be any that keep to these rules, and one draw needn't show every extreme that they name: Part 0 is the high-noise group, with a timestep from 875 to 999; part 1 the low-noise group, with one from 0 to 874.
All inputs are finite; a program needn't handle non-finite values.
Results may differ from a plain program's by a relative error of at most 0.012.
The roundings to bfloat16 on the way count: a program that leaves them out, or rounds other values in their place, can miss the bound.
Values may be sent and summed in bfloat16 or wider, within the bound.
A program may use at most 384 MiB of HBM per device.

v0:
```python
import math
import jax
import jax.numpy as jnp
from jax import lax
from jax.sharding import PartitionSpec as P

HEAD_DIM = 128
FREQ = 256
HGT = 32
WID = 32
EPSILON = 1e-06


def rms_normed(tensor, gain_vector):
    mean_square = jnp.mean(tensor * tensor, axis=-1, keepdims=True)
    return tensor * lax.rsqrt(mean_square + EPSILON) * gain_vector


def rotate_pairs(tensor, positions):
    half_dim = HEAD_DIM // 2
    sixth = HEAD_DIM // 6
    frame_pairs = (HEAD_DIM - 4 * sixth) // 2
    pair_index = jnp.arange(half_dim, dtype=jnp.int32)
    in_frame = pair_index < frame_pairs
    in_height = (pair_index >= frame_pairs) & (pair_index < frame_pairs + sixth)
    local_index = jnp.where(
        in_frame,
        pair_index,
        jnp.where(in_height, pair_index - frame_pairs, pair_index - frame_pairs - sixth),
    )
    segment_dims = jnp.where(in_frame, 2 * frame_pairs, 2 * sixth)
    inverse = jnp.power(
        jnp.float32(10000.0),
        -2.0 * local_index.astype(jnp.float32) / segment_dims.astype(jnp.float32),
    )
    frame_at = positions // (HGT * WID)
    height_at = positions // WID % HGT
    width_at = positions % WID
    coordinate = jnp.where(
        in_frame[None, :],
        frame_at[:, None],
        jnp.where(in_height[None, :], height_at[:, None], width_at[:, None]),
    ).astype(jnp.float32)
    angle_table = coordinate * inverse[None, :]
    cosine = jnp.cos(angle_table)[:, None, :]
    sine_table = jnp.sin(angle_table)[:, None, :]
    paired = tensor.reshape(tensor.shape[0], tensor.shape[1], half_dim, 2)
    even_part = paired[..., 0]
    odd_part = paired[..., 1]
    turned = jnp.stack(
        [even_part * cosine - odd_part * sine_table, even_part * sine_table + odd_part * cosine],
        axis=-1,
    )
    return turned.reshape(tensor.shape)


def prepare(tensor, gain_vector, positions):
    normed = rms_normed(tensor.astype(jnp.float32), gain_vector)
    head_total = tensor.shape[1] // HEAD_DIM
    turned = rotate_pairs(normed.reshape(tensor.shape[0], head_total, HEAD_DIM), positions)
    return turned.reshape(tensor.shape).astype(jnp.bfloat16)


def gate_vector(timestep, base_slice, weight_slice):
    half_freq = FREQ // 2
    exponent = jnp.arange(half_freq, dtype=jnp.int32).astype(jnp.float32) / half_freq
    frequency = jnp.power(jnp.float32(10000.0), -exponent)
    phase = timestep.astype(jnp.float32)[:, None] * frequency[None, :]
    embedded = jnp.concatenate([jnp.cos(phase), jnp.sin(phase)], axis=1)
    projected = jnp.dot(
        embedded, weight_slice, precision=lax.Precision.HIGHEST, preferred_element_type=jnp.float32
    )
    return base_slice + projected[0]


def initial_state(query_count, heads_here):
    running_max = jnp.full((heads_here, query_count), -1e30, jnp.float32)
    running_total = jnp.zeros((heads_here, query_count), jnp.float32)
    accumulated = jnp.zeros((query_count, heads_here, HEAD_DIM), jnp.float32)
    return (running_max, running_total, accumulated)


def attend_keys(softmax_state, query_heads, key_piece, value_piece):
    query_count = query_heads.shape[0]
    heads_here = query_heads.shape[1] // HEAD_DIM
    query_view = query_heads.reshape(query_count, heads_here, HEAD_DIM)
    key_count = key_piece.shape[0]
    block_size = math.gcd(key_count, 1024)
    key_view = key_piece.reshape(key_count // block_size, block_size, heads_here, HEAD_DIM)
    value_view = value_piece.reshape(key_count // block_size, block_size, heads_here, HEAD_DIM)
    score_scale = 1.0 / math.sqrt(HEAD_DIM)

    def advance(running, blocks):
        running_max, running_total, accumulated = running
        key_block, value_block = blocks
        scores = (
            jnp.einsum("qhd,khd->hqk", query_view, key_block, preferred_element_type=jnp.float32)
            * score_scale
        )
        new_max = jnp.maximum(running_max, jnp.max(scores, axis=2))
        shrink = jnp.exp(running_max - new_max)
        exponent_values = jnp.exp(scores - new_max[:, :, None])
        new_total = running_total * shrink + jnp.sum(exponent_values, axis=2)
        weights = exponent_values.astype(jnp.bfloat16)
        update = jnp.einsum(
            "hqk,khd->qhd", weights, value_block, preferred_element_type=jnp.float32
        )
        new_accumulated = accumulated * jnp.transpose(shrink)[:, :, None] + update
        return ((new_max, new_total, new_accumulated), None)

    softmax_state, unused = lax.scan(advance, softmax_state, (key_view, value_view))
    return softmax_state


def local(queries, keys, values, query_gain, key_gain, timestep, gate_base, time_weight):
    token_count = queries.shape[0]
    width_total = queries.shape[1]
    seq_count = lax.axis_size("seq")
    fsdp_count = lax.axis_size("fsdp")
    block_index = lax.axis_index("seq") * fsdp_count + lax.axis_index("fsdp")
    positions = block_index * token_count + jnp.arange(token_count, dtype=jnp.int32)
    query_rot = prepare(queries, query_gain, positions)
    key_rot = prepare(keys, key_gain, positions)
    group_width = width_total // seq_count
    heads_here = group_width // HEAD_DIM
    group_start = lax.axis_index("seq") * group_width
    base_slice = lax.dynamic_slice_in_dim(gate_base, group_start, group_width, 0)
    weight_slice = lax.dynamic_slice_in_dim(time_weight, group_start, group_width, 1)
    gate_slice = gate_vector(timestep, base_slice, weight_slice)
    query_heads, key_heads, value_heads = (
        lax.all_to_all(query_rot, "seq", split_axis=1, concat_axis=0, tiled=True),
        lax.all_to_all(key_rot, "seq", split_axis=1, concat_axis=0, tiled=True),
        lax.all_to_all(values, "seq", split_axis=1, concat_axis=0, tiled=True),
    )
    softmax_state = initial_state(query_heads.shape[0], heads_here)
    softmax_state = attend_keys(
        softmax_state,
        query_heads,
        lax.all_gather(key_heads, "fsdp", axis=0, tiled=True),
        lax.all_gather(value_heads, "fsdp", axis=0, tiled=True),
    )
    running_max, running_total, accumulated = softmax_state
    heads_out = accumulated / jnp.transpose(running_total)[:, :, None]
    gated = (heads_out.reshape(heads_out.shape[0], group_width) * gate_slice[None, :]).astype(
        jnp.bfloat16
    )
    return lax.all_to_all(gated, "seq", split_axis=0, concat_axis=1, tiled=True)


def solution(mesh):
    return jax.shard_map(
        local,
        mesh=mesh,
        in_specs=(
            P(("expert", "seq", "fsdp"), None),
            P(("expert", "seq", "fsdp"), None),
            P(("expert", "seq", "fsdp"), None),
            P("expert"),
            P("expert"),
            P("expert"),
            P("expert"),
            P("expert", None),
        ),
        out_specs=P(("expert", "seq", "fsdp"), None),
        check_vma=False,
    )
```

profile of v0, /device:TPU:0, one launch (start us, length us, event | category | flops | bytes accessed | tf_op | source)
XLA Modules:
  0.0 1656.6 jit_solution(9292958395011838681)
XLA Ops:
  132.2 123.6 %all_to_all.64 = bf16[512,4,1280]{0,2,1:T(8,128)(2,1)} all-to-all(bf16[512,4,1280]{0,2,1:T(8,128)(2,1)} %convert_element_type.71), channel_id=1, replica_groups=mesh['expert'=2,'seq'=4,'fsdp'=4] {'seq'}, dimensions={1} | all-to-all | bytes 10485760 | tf_op jit(solution)/shard_map/all_to_all | solution.py:132
  271.7 121.5 %all_to_all.65 = bf16[512,4,1280]{0,2,1:T(8,128)(2,1)} all-to-all(bf16[512,4,1280]{0,2,1:T(8,128)(2,1)} %bitcast.73), channel_id=1, replica_groups=mesh['expert'=2,'seq'=4,'fsdp'=4] {'seq'}, dimensions={1} | all-to-all | bytes 10485760 | tf_op jit(solution)/shard_map/all_to_all | solution.py:133
  432.6 110.6 %all-to-all-done.1 = bf16[512,4,1280]{0,2,1:T(8,128)(2,1)} async-done(((bf16[512,4,1280]{0,2,1:T(8,128)(2,1)}), bf16[512,4,1280]{0,2,1:T(8,128)(2,1)}, u32[]{:S(2)}, u32[]{:S(2)}) %all-to-all-start.1) | async-done | bytes 5242912 | tf_op jit(solution)/shard_map/all_to_all | solution.py:131
  569.5 40.7 %reshape.322 = bf16[8,1024,10,128]{3,2,1,0:T(8,128)(2,1)} reshape(bf16[8192,1280]{1,0:T(8,128)(2,1)} %all-gather.3.cloned.1.call-done) | data formatting | bytes 41943040 | tf_op jit(solution)/shard_map/reshape | solution.py:89
  632.9 40.7 %reshape.323 = bf16[8,1024,10,128]{3,2,1,0:T(8,128)(2,1)} reshape(bf16[8192,1280]{1,0:T(8,128)(2,1)} %all-gather.5.cloned.1.call-done) | data formatting | bytes 41943040 | tf_op jit(solution)/shard_map/reshape | solution.py:90
  673.6 43.1 %copy.59 = bf16[8,1024,10,128]{1,3,2,0:T(8,128)(2,1)} copy(bf16[8,1024,10,128]{3,2,1,0:T(8,128)(2,1)} %reshape.323) | data formatting | bytes 41943040
  716.7 753.8 %while.15 = (s32[]{:T(128)}, f32[10,2048]{1,0:T(8,128)S(1)}, f32[10,2048]{1,0:T(8,128)S(1)}, f32[2048,10,128]{0,2,1:T(8,128)}, bf16[8,1024,10,128]{3,1,2,0:T(8,1...) while((s32[]{:T(128)}, f32[10,2048]{1,0:T(8,128)S(1)}, ...), condition=%wide.region_5.6_spmd.clone, body=%wide.region_2.5_spmd.clone.sunk | while | flops 10913177600 | bytes 284427360 | solution.py:111
  716.7 31.8 %bitcast_reduce_fusion.2 = (f32[10,2048]{1,0:T(8,128)S(1)}, f32[10,1024,2048]{2,1,0:T(8,128)}) fusion(bf16[2048,10,128]{2,0,1:T(8,128)(2,1)} %get-tuple-element.203, bf16[8,1024,10,128]{3,1,2,0:T(8,128)(2,1)} %get-tuple-element.202, s32[]{:T(128)} %get-tuple-element.189), kind=kOutput, calls=%fused_computation.1.clone.1 | convolution fusion | flops 5410631680 | bytes 91832832 | tf_op jit(solution)/shard_map/while/body/eval_jaxpr/qhd,khd->hqk/dot_general | solution.py:97
  748.5 33.6 %bitcast_add_fusion.2 = f32[2048,10,128]{0,2,1:T(8,128)} fusion(f32[2048,10,128]{0,2,1:T(8,128)} %get-tuple-element.192, f32[2048,10]{0,1:T(8,128)S(1)} %get-tuple-element.179, pred[]{:T(512)S(6)} %compare.24, f32[10,1024,2048]{2,1,0:T(8,128)} %get-tuple-element.178, f32[10,2048]{1,0:T(8,128)S(1)} %get-tuple-element.199, ...), kind=kOutput, calls=%fused_computation.8.clone.1 | convolution fusion | flops 5439488000 | bytes 107643392 | tf_op jit(solution)/shard_map/while/body/eval_jaxpr/hqk,khd->qhd/dot_general | solution.py:105
  808.3 31.8 %bitcast_reduce_fusion.2 = (f32[10,2048]{1,0:T(8,128)S(1)}, f32[10,1024,2048]{2,1,0:T(8,128)}) fusion(bf16[2048,10,128]{2,0,1:T(8,128)(2,1)} %get-tuple-element.203, bf16[8,1024,10,128]{3,1,2,0:T(8,128)(2,1)} %get-tuple-element.202, s32[]{:T(128)} %get-tuple-element.189), kind=kOutput, calls=%fused_computation.1.clone.1 | convolution fusion | flops 5410631680 | bytes 91832832 | tf_op jit(solution)/shard_map/while/body/eval_jaxpr/qhd,khd->hqk/dot_general | solution.py:97
  840.1 36.5 %bitcast_add_fusion.2 = f32[2048,10,128]{0,2,1:T(8,128)} fusion(f32[2048,10,128]{0,2,1:T(8,128)} %get-tuple-element.192, f32[2048,10]{0,1:T(8,128)S(1)} %get-tuple-element.179, pred[]{:T(512)S(6)} %compare.24, f32[10,1024,2048]{2,1,0:T(8,128)} %get-tuple-element.178, f32[10,2048]{1,0:T(8,128)S(1)} %get-tuple-element.199, ...), kind=kOutput, calls=%fused_computation.8.clone.1 | convolution fusion | flops 5439488000 | bytes 107643392 | tf_op jit(solution)/shard_map/while/body/eval_jaxpr/hqk,khd->qhd/dot_general | solution.py:105
  902.8 31.8 %bitcast_reduce_fusion.2 = (f32[10,2048]{1,0:T(8,128)S(1)}, f32[10,1024,2048]{2,1,0:T(8,128)}) fusion(bf16[2048,10,128]{2,0,1:T(8,128)(2,1)} %get-tuple-element.203, bf16[8,1024,10,128]{3,1,2,0:T(8,128)(2,1)} %get-tuple-element.202, s32[]{:T(128)} %get-tuple-element.189), kind=kOutput, calls=%fused_computation.1.clone.1 | convolution fusion | flops 5410631680 | bytes 91832832 | tf_op jit(solution)/shard_map/while/body/eval_jaxpr/qhd,khd->hqk/dot_general | solution.py:97
  934.7 36.5 %bitcast_add_fusion.2 = f32[2048,10,128]{0,2,1:T(8,128)} fusion(f32[2048,10,128]{0,2,1:T(8,128)} %get-tuple-element.192, f32[2048,10]{0,1:T(8,128)S(1)} %get-tuple-element.179, pred[]{:T(512)S(6)} %compare.24, f32[10,1024,2048]{2,1,0:T(8,128)} %get-tuple-element.178, f32[10,2048]{1,0:T(8,128)S(1)} %get-tuple-element.199, ...), kind=kOutput, calls=%fused_computation.8.clone.1 | convolution fusion | flops 5439488000 | bytes 107643392 | tf_op jit(solution)/shard_map/while/body/eval_jaxpr/hqk,khd->qhd/dot_general | solution.py:105
  997.4 31.8 %bitcast_reduce_fusion.2 = (f32[10,2048]{1,0:T(8,128)S(1)}, f32[10,1024,2048]{2,1,0:T(8,128)}) fusion(bf16[2048,10,128]{2,0,1:T(8,128)(2,1)} %get-tuple-element.203, bf16[8,1024,10,128]{3,1,2,0:T(8,128)(2,1)} %get-tuple-element.202, s32[]{:T(128)} %get-tuple-element.189), kind=kOutput, calls=%fused_computation.1.clone.1 | convolution fusion | flops 5410631680 | bytes 91832832 | tf_op jit(solution)/shard_map/while/body/eval_jaxpr/qhd,khd->hqk/dot_general | solution.py:97
  1029.3 36.5 %bitcast_add_fusion.2 = f32[2048,10,128]{0,2,1:T(8,128)} fusion(f32[2048,10,128]{0,2,1:T(8,128)} %get-tuple-element.192, f32[2048,10]{0,1:T(8,128)S(1)} %get-tuple-element.179, pred[]{:T(512)S(6)} %compare.24, f32[10,1024,2048]{2,1,0:T(8,128)} %get-tuple-element.178, f32[10,2048]{1,0:T(8,128)S(1)} %get-tuple-element.199, ...), kind=kOutput, calls=%fused_computation.8.clone.1 | convolution fusion | flops 5439488000 | bytes 107643392 | tf_op jit(solution)/shard_map/while/body/eval_jaxpr/hqk,khd->qhd/dot_general | solution.py:105
  1092.0 31.8 %bitcast_reduce_fusion.2 = (f32[10,2048]{1,0:T(8,128)S(1)}, f32[10,1024,2048]{2,1,0:T(8,128)}) fusion(bf16[2048,10,128]{2,0,1:T(8,128)(2,1)} %get-tuple-element.203, bf16[8,1024,10,128]{3,1,2,0:T(8,128)(2,1)} %get-tuple-element.202, s32[]{:T(128)} %get-tuple-element.189), kind=kOutput, calls=%fused_computation.1.clone.1 | convolution fusion | flops 5410631680 | bytes 91832832 | tf_op jit(solution)/shard_map/while/body/eval_jaxpr/qhd,khd->hqk/dot_general | solution.py:97
  1123.8 36.5 %bitcast_add_fusion.2 = f32[2048,10,128]{0,2,1:T(8,128)} fusion(f32[2048,10,128]{0,2,1:T(8,128)} %get-tuple-element.192, f32[2048,10]{0,1:T(8,128)S(1)} %get-tuple-element.179, pred[]{:T(512)S(6)} %compare.24, f32[10,1024,2048]{2,1,0:T(8,128)} %get-tuple-element.178, f32[10,2048]{1,0:T(8,128)S(1)} %get-tuple-element.199, ...), kind=kOutput, calls=%fused_computation.8.clone.1 | convolution fusion | flops 5439488000 | bytes 107643392 | tf_op jit(solution)/shard_map/while/body/eval_jaxpr/hqk,khd->qhd/dot_general | solution.py:105
  1186.6 31.8 %bitcast_reduce_fusion.2 = (f32[10,2048]{1,0:T(8,128)S(1)}, f32[10,1024,2048]{2,1,0:T(8,128)}) fusion(bf16[2048,10,128]{2,0,1:T(8,128)(2,1)} %get-tuple-element.203, bf16[8,1024,10,128]{3,1,2,0:T(8,128)(2,1)} %get-tuple-element.202, s32[]{:T(128)} %get-tuple-element.189), kind=kOutput, calls=%fused_computation.1.clone.1 | convolution fusion | flops 5410631680 | bytes 91832832 | tf_op jit(solution)/shard_map/while/body/eval_jaxpr/qhd,khd->hqk/dot_general | solution.py:97
  1218.4 36.5 %bitcast_add_fusion.2 = f32[2048,10,128]{0,2,1:T(8,128)} fusion(f32[2048,10,128]{0,2,1:T(8,128)} %get-tuple-element.192, f32[2048,10]{0,1:T(8,128)S(1)} %get-tuple-element.179, pred[]{:T(512)S(6)} %compare.24, f32[10,1024,2048]{2,1,0:T(8,128)} %get-tuple-element.178, f32[10,2048]{1,0:T(8,128)S(1)} %get-tuple-element.199, ...), kind=kOutput, calls=%fused_computation.8.clone.1 | convolution fusion | flops 5439488000 | bytes 107643392 | tf_op jit(solution)/shard_map/while/body/eval_jaxpr/hqk,khd->qhd/dot_general | solution.py:105
  1281.1 31.8 %bitcast_reduce_fusion.2 = (f32[10,2048]{1,0:T(8,128)S(1)}, f32[10,1024,2048]{2,1,0:T(8,128)}) fusion(bf16[2048,10,128]{2,0,1:T(8,128)(2,1)} %get-tuple-element.203, bf16[8,1024,10,128]{3,1,2,0:T(8,128)(2,1)} %get-tuple-element.202, s32[]{:T(128)} %get-tuple-element.189), kind=kOutput, calls=%fused_computation.1.clone.1 | convolution fusion | flops 5410631680 | bytes 91832832 | tf_op jit(solution)/shard_map/while/body/eval_jaxpr/qhd,khd->hqk/dot_general | solution.py:97
  1313.0 36.5 %bitcast_add_fusion.2 = f32[2048,10,128]{0,2,1:T(8,128)} fusion(f32[2048,10,128]{0,2,1:T(8,128)} %get-tuple-element.192, f32[2048,10]{0,1:T(8,128)S(1)} %get-tuple-element.179, pred[]{:T(512)S(6)} %compare.24, f32[10,1024,2048]{2,1,0:T(8,128)} %get-tuple-element.178, f32[10,2048]{1,0:T(8,128)S(1)} %get-tuple-element.199, ...), kind=kOutput, calls=%fused_computation.8.clone.1 | convolution fusion | flops 5439488000 | bytes 107643392 | tf_op jit(solution)/shard_map/while/body/eval_jaxpr/hqk,khd->qhd/dot_general | solution.py:105
  1375.7 31.8 %bitcast_reduce_fusion.2 = (f32[10,2048]{1,0:T(8,128)S(1)}, f32[10,1024,2048]{2,1,0:T(8,128)}) fusion(bf16[2048,10,128]{2,0,1:T(8,128)(2,1)} %get-tuple-element.203, bf16[8,1024,10,128]{3,1,2,0:T(8,128)(2,1)} %get-tuple-element.202, s32[]{:T(128)} %get-tuple-element.189), kind=kOutput, calls=%fused_computation.1.clone.1 | convolution fusion | flops 5410631680 | bytes 91832832 | tf_op jit(solution)/shard_map/while/body/eval_jaxpr/qhd,khd->hqk/dot_general | solution.py:97
  1407.6 36.5 %bitcast_add_fusion.2 = f32[2048,10,128]{0,2,1:T(8,128)} fusion(f32[2048,10,128]{0,2,1:T(8,128)} %get-tuple-element.192, f32[2048,10]{0,1:T(8,128)S(1)} %get-tuple-element.179, pred[]{:T(512)S(6)} %compare.24, f32[10,1024,2048]{2,1,0:T(8,128)} %get-tuple-element.178, f32[10,2048]{1,0:T(8,128)S(1)} %get-tuple-element.199, ...), kind=kOutput, calls=%fused_computation.8.clone.1 | convolution fusion | flops 5439488000 | bytes 107643392 | tf_op jit(solution)/shard_map/while/body/eval_jaxpr/hqk,khd->qhd/dot_general | solution.py:105
  1512.8 121.2 %all_to_all.66 = bf16[4,512,1280]{2,1,0:T(8,128)(2,1)} all-to-all(bf16[4,512,1280]{2,1,0:T(8,128)(2,1)} %copy.60), channel_id=1, replica_groups=mesh['expert'=2,'seq'=4,'fsdp'=4] {'seq'}, dimensions={0} | all-to-all | bytes 10485760 | tf_op jit(solution)/shard_map/all_to_all | solution.py:147
  (82 shorter events, 496.7 us)
Async XLA Ops:
  6.5 563.0 %all-gather.3.cloned.1.call-start = ((), (), s32[]{:S(2)}) async-start(), calls=%async_computation.4 | async-start | bytes 26214400 | tf_op jit(solution)/shard_map/all_gather | solution.py:139
  29.7 16.5 copy-start.1
  263.7 369.2 %all-gather.5.cloned.1.call-start = ((), (), s32[]{:S(2)}) async-start(), calls=%async_computation.5 | async-start | bytes 26214400 | tf_op jit(solution)/shard_map/all_gather | solution.py:140
  423.3 119.9 %all-to-all-start.1 = ((bf16[512,4,1280]{0,2,1:T(8,128)(2,1)}), bf16[512,4,1280]{0,2,1:T(8,128)(2,1)}, u32[]{:S(2)}, u32[]{:S(2)}) async-start(bf16[512,4,1280]{0,2,1:T(8,128)(2,1)} %convert_element_type.73), calls=%async_computation.1 | async-start | bytes 10485760 | tf_op jit(solution)/shard_map/all_to_all | solution.py:131
  1480.8 13.2 copy-start
Sparse Core Ops, SparseCore 0:
  263.8 130.5 all-gather.2
  401.3 130.5 all-gather.4
where the time goes:
time: 1660 us
  matrix products  546 us (33%)
  blocking collectives  366 us (22%)
  other arithmetic  312 us (19%)
  local copies, waits for them, and re-layouts  302 us (18%)
  waiting for transfers between devices  111 us (7%)
    dot_general x8, matrix products, advance(): jnp.einsum('hqk,khd->qhd', weights, value_block, preferred_element_type=j...  289 us
    dot_general x8, matrix products, advance(): jnp.einsum('qhd,khd->hqk', query_view, key_block, preferred_element_type=...  255 us
    reduce_sum x8, other arithmetic, advance(): new_total = running_total * shrink + jnp.sum(exponent_values, axis=2)  209 us
    all_to_all x1, blocking collectives, local(): lax.all_to_all(key_rot, 'seq', split_axis=1, concat_axis=0, tiled=True)  124 us
    all_to_all x1, blocking collectives, local(): lax.all_to_all(values, 'seq', split_axis=1, concat_axis=0, tiled=True)  122 us
    all_to_all x1, blocking collectives, local(): return lax.all_to_all(gated, 'seq', split_axis=0, concat_axis=1, tiled=True)  121 us
    all_to_all x1, waiting for transfers between devices, local(): lax.all_to_all(query_rot, 'seq', split_axis=1, concat_axis=0, tiled=True)  111 us
    unnamed x8, local copies, waits for them, and re-layouts  81.6 us
  transfers between devices with their start and end apart: 3, of which 1 were waited for; matrix products, arithmetic and copies ran while one was open for 8% of the time, Pallas kernels for 0%

commit v1 on v0

--- a/solution.py
+++ b/solution.py
@@ -9,6 +9,22 @@
 HGT = 32
 WID = 32
 EPSILON = 1e-06
+
+
+def exchange_in_pairs(array, axis, split, join):
+    ways, here = (lax.axis_size(axis), lax.axis_index(axis))
+    width = array.shape[split] // ways
+    lengths = list(array.shape)
+    lengths[split] = width
+    height = lengths[join]
+    lengths[join] = height * ways
+    full = jnp.zeros(lengths, array.dtype)
+    for mask in range(ways):
+        part = lax.dynamic_slice_in_dim(array, (here ^ mask) * width, width, axis=split)
+        if mask:
+            part = lax.ppermute(part, axis, [(d, d ^ mask) for d in range(ways)])
+        full = lax.dynamic_update_slice_in_dim(full, part, (here ^ mask) * height, axis=join)
+    return full
 
 
 def rms_normed(tensor, gain_vector):
@@ -130,7 +146,7 @@
     query_heads, key_heads, value_heads = (
         lax.all_to_all(query_rot, "seq", split_axis=1, concat_axis=0, tiled=True),
         lax.all_to_all(key_rot, "seq", split_axis=1, concat_axis=0, tiled=True),
-        lax.all_to_all(values, "seq", split_axis=1, concat_axis=0, tiled=True),
+        exchange_in_pairs(values, "seq", 1, 0),
     )
     softmax_state = initial_state(query_heads.shape[0], heads_here)
     softmax_state = attend_keys(

time: 1660 us -> 1610 us (0.970)
  blocking collectives: 366 us -> 263 us
  waiting for transfers between devices: 111 us -> 192 us
  local copies, waits for them, and re-layouts: 302 us -> 266 us
    all_to_all x1 -> x0, blocking collectives: 122 us -> none  [local(): lax.all_to_all(values, 'seq', split_axis=1, concat_axis=0, tiled=True)]
    ppermute x0 -> x3, waiting for transfers between devices: none -> 79.9 us  [exchange_in_pairs(): part = lax.ppermute(part, axis, [(d, d ^ mask) for d in range(ways)])]
    reshape x1 -> x0, local copies, waits for them, and re-layouts: 40.7 us -> none  [attend_keys(): value_piece.reshape(key_count // block_size, block_size, heads_here, HEAD...]
    all_to_all x1, blocking collectives: 124 us -> 142 us  [local(): lax.all_to_all(key_rot, 'seq', split_axis=1, concat_axis=0, tiled=True)]
    unnamed x8 -> x10, local copies, waits for them, and re-layouts: 81.6 us -> 75.7 us
  transfers between devices with their start and end apart: 3 -> 6, of which waited for: 1 -> 3; matrix products, arithmetic and copies ran while one was open for 8% -> 15% of each run, Pallas kernels for 0% -> 0%
where the time goes in v1:
time: 1610 us
  matrix products  546 us (34%)
  other arithmetic  314 us (20%)
  local copies, waits for them, and re-layouts  266 us (17%)
  blocking collectives  263 us (16%)
  waiting for transfers between devices  192 us (12%)
    dot_general x8, matrix products, advance(): jnp.einsum('hqk,khd->qhd', weights, value_block, preferred_element_type=j...  289 us
    dot_general x8, matrix products, advance(): jnp.einsum('qhd,khd->hqk', query_view, key_block, preferred_element_type=...  255 us
    reduce_sum x8, other arithmetic, advance(): new_total = running_total * shrink + jnp.sum(exponent_values, axis=2)  209 us
    all_to_all x1, blocking collectives, local(): lax.all_to_all(key_rot, 'seq', split_axis=1, concat_axis=0, tiled=True)  142 us
    all_to_all x1, blocking collectives, local(): return lax.all_to_all(gated, 'seq', split_axis=0, concat_axis=1, tiled=True)  121 us
    all_to_all x1, waiting for transfers between devices, local(): lax.all_to_all(query_rot, 'seq', split_axis=1, concat_axis=0, tiled=True)  112 us
    ppermute x3, waiting for transfers between devices, exchange_in_pairs(): part = lax.ppermute(part, axis, [(d, d ^ mask) for d in range(ways)])  79.9 us
    unnamed x10, local copies, waits for them, and re-layouts  75.7 us
  transfers between devices with their start and end apart: 6, of which 3 were waited for; matrix products, arithmetic and copies ran while one was open for 15% of the time, Pallas kernels for 0%

profile of v1, /device:TPU:0, one launch (start us, length us, event | category | flops | bytes accessed | tf_op | source)
XLA Modules:
  0.0 1607.0 jit_solution(10574533252239122612)
XLA Ops:
  21.6 48.9 %collective-permute-done = bf16[512,1280]{1,0:T(8,128)(2,1)} collective-permute-done((bf16[512,1280]{1,0:T(8,128)(2,1)}, bf16[512,1280]{1,0:T(8,128)(2,1)}, u32[]{:S(2)}, u32[]{:S(2)}) %collective-permute-start) | collective-permute-done | bytes 1310752 | tf_op jit(solution)/shard_map/ppermute | solution.py:25
  72.2 31.0 %collective-permute-done.1 = bf16[512,1280]{1,0:T(8,128)(2,1)} collective-permute-done((bf16[512,1280]{1,0:T(8,128)(2,1)}, bf16[512,1280]{1,0:T(8,128)(2,1)}, u32[]{:S(2)}, u32[]{:S(2)}) %collective-permute-start.1) | collective-permute-done | bytes 1310752 | tf_op jit(solution)/shard_map/ppermute | solution.py:25
  185.8 31.5 %subtract_convert_fusion = (bf16[512,40,64,1]{0,3,2,1:T(2,128)(2,1)}, bf16[512,40,64,1]{0,3,2,1:T(2,128)(2,1)}, bf16[512,40,64,1]{0,3,2,1:T(2,128)(2,1)}, bf16[512,40,64,1]{0,3,2,1:T(2,128)(2,1)}) fusion(f32[512,40,64,2]{0,3,2,1:T(2,128)} %reshape_reshape.9, f32[512,64]{0,1:T(8,128)S(1)} %get-tuple-element.119, f32[512,64]{0,1:T(8,128)S(1)} %get-tuple-element.118, ...), kind=kLoop, calls=%fused_computation.36 | loop fusion | flops 20971520 | bytes 31719424 | tf_op jit(solution)/shard_map/convert
  239.1 141.8 %all_to_all.45 = bf16[512,4,1280]{0,2,1:T(8,128)(2,1)} all-to-all(bf16[512,4,1280]{0,2,1:T(8,128)(2,1)} %convert_element_type.71), channel_id=1, replica_groups=mesh['expert'=2,'seq'=4,'fsdp'=4] {'seq'}, dimensions={1} | all-to-all | bytes 10485760 | tf_op jit(solution)/shard_map/all_to_all | solution.py:148
  420.2 111.7 %all-to-all-done.1 = bf16[512,4,1280]{0,2,1:T(8,128)(2,1)} async-done(((bf16[512,4,1280]{0,2,1:T(8,128)(2,1)}), bf16[512,4,1280]{0,2,1:T(8,128)(2,1)}, u32[]{:S(2)}, u32[]{:S(2)}) %all-to-all-start.1) | async-done | bytes 5242912 | tf_op jit(solution)/shard_map/all_to_all | solution.py:147
  603.5 40.7 %reshape.319 = bf16[8,1024,10,128]{3,2,1,0:T(8,128)(2,1)} reshape(bf16[8192,1280]{1,0:T(8,128)(2,1)} %all-gather.3.cloned.1.call-done) | data formatting | bytes 41943040 | tf_op jit(solution)/shard_map/reshape | solution.py:105
  666.8 754.0 %while.15 = (s32[]{:T(128)}, f32[10,2048]{1,0:T(8,128)S(1)}, f32[10,2048]{1,0:T(8,128)S(1)}, f32[2048,10,128]{0,2,1:T(8,128)}, bf16[8,1024,10,128]{3,1,2,0:T(8,1...) while((s32[]{:T(128)}, f32[10,2048]{1,0:T(8,128)S(1)}, ...), condition=%wide.region_5.6_spmd.clone, body=%wide.region_2.5_spmd.clone.sunk | while | flops 10913177600 | bytes 284427360 | solution.py:127
  666.8 31.8 %bitcast_reduce_fusion.2 = (f32[10,2048]{1,0:T(8,128)S(1)}, f32[10,1024,2048]{2,1,0:T(8,128)}) fusion(bf16[2048,10,128]{2,0,1:T(8,128)(2,1)} %get-tuple-element.200, bf16[8,1024,10,128]{3,1,2,0:T(8,128)(2,1)} %get-tuple-element.199, s32[]{:T(128)} %get-tuple-element.186), kind=kOutput, calls=%fused_computation.1.clone.1 | convolution fusion | flops 5410631680 | bytes 91832832 | tf_op jit(solution)/shard_map/while/body/eval_jaxpr/qhd,khd->hqk/dot_general | solution.py:113
  698.7 33.6 %bitcast_add_fusion.2 = f32[2048,10,128]{0,2,1:T(8,128)} fusion(f32[2048,10,128]{0,2,1:T(8,128)} %get-tuple-element.189, f32[2048,10]{0,1:T(8,128)S(1)} %get-tuple-element.176, pred[]{:T(512)S(6)} %compare.24, f32[10,1024,2048]{2,1,0:T(8,128)} %get-tuple-element.175, f32[10,2048]{1,0:T(8,128)S(1)} %get-tuple-element.196, ...), kind=kOutput, calls=%fused_computation.8.clone.1 | convolution fusion | flops 5439488000 | bytes 107643392 | tf_op jit(solution)/shard_map/while/body/eval_jaxpr/hqk,khd->qhd/dot_general | solution.py:121
  758.5 31.8 %bitcast_reduce_fusion.2 = (f32[10,2048]{1,0:T(8,128)S(1)}, f32[10,1024,2048]{2,1,0:T(8,128)}) fusion(bf16[2048,10,128]{2,0,1:T(8,128)(2,1)} %get-tuple-element.200, bf16[8,1024,10,128]{3,1,2,0:T(8,128)(2,1)} %get-tuple-element.199, s32[]{:T(128)} %get-tuple-element.186), kind=kOutput, calls=%fused_computation.1.clone.1 | convolution fusion | flops 5410631680 | bytes 91832832 | tf_op jit(solution)/shard_map/while/body/eval_jaxpr/qhd,khd->hqk/dot_general | solution.py:113
  790.3 36.5 %bitcast_add_fusion.2 = f32[2048,10,128]{0,2,1:T(8,128)} fusion(f32[2048,10,128]{0,2,1:T(8,128)} %get-tuple-element.189, f32[2048,10]{0,1:T(8,128)S(1)} %get-tuple-element.176, pred[]{:T(512)S(6)} %compare.24, f32[10,1024,2048]{2,1,0:T(8,128)} %get-tuple-element.175, f32[10,2048]{1,0:T(8,128)S(1)} %get-tuple-element.196, ...), kind=kOutput, calls=%fused_computation.8.clone.1 | convolution fusion | flops 5439488000 | bytes 107643392 | tf_op jit(solution)/shard_map/while/body/eval_jaxpr/hqk,khd->qhd/dot_general | solution.py:121
  853.1 31.8 %bitcast_reduce_fusion.2 = (f32[10,2048]{1,0:T(8,128)S(1)}, f32[10,1024,2048]{2,1,0:T(8,128)}) fusion(bf16[2048,10,128]{2,0,1:T(8,128)(2,1)} %get-tuple-element.200, bf16[8,1024,10,128]{3,1,2,0:T(8,128)(2,1)} %get-tuple-element.199, s32[]{:T(128)} %get-tuple-element.186), kind=kOutput, calls=%fused_computation.1.clone.1 | convolution fusion | flops 5410631680 | bytes 91832832 | tf_op jit(solution)/shard_map/while/body/eval_jaxpr/qhd,khd->hqk/dot_general | solution.py:113
  885.0 36.5 %bitcast_add_fusion.2 = f32[2048,10,128]{0,2,1:T(8,128)} fusion(f32[2048,10,128]{0,2,1:T(8,128)} %get-tuple-element.189, f32[2048,10]{0,1:T(8,128)S(1)} %get-tuple-element.176, pred[]{:T(512)S(6)} %compare.24, f32[10,1024,2048]{2,1,0:T(8,128)} %get-tuple-element.175, f32[10,2048]{1,0:T(8,128)S(1)} %get-tuple-element.196, ...), kind=kOutput, calls=%fused_computation.8.clone.1 | convolution fusion | flops 5439488000 | bytes 107643392 | tf_op jit(solution)/shard_map/while/body/eval_jaxpr/hqk,khd->qhd/dot_general | solution.py:121
  947.7 31.8 %bitcast_reduce_fusion.2 = (f32[10,2048]{1,0:T(8,128)S(1)}, f32[10,1024,2048]{2,1,0:T(8,128)}) fusion(bf16[2048,10,128]{2,0,1:T(8,128)(2,1)} %get-tuple-element.200, bf16[8,1024,10,128]{3,1,2,0:T(8,128)(2,1)} %get-tuple-element.199, s32[]{:T(128)} %get-tuple-element.186), kind=kOutput, calls=%fused_computation.1.clone.1 | convolution fusion | flops 5410631680 | bytes 91832832 | tf_op jit(solution)/shard_map/while/body/eval_jaxpr/qhd,khd->hqk/dot_general | solution.py:113
  979.6 36.5 %bitcast_add_fusion.2 = f32[2048,10,128]{0,2,1:T(8,128)} fusion(f32[2048,10,128]{0,2,1:T(8,128)} %get-tuple-element.189, f32[2048,10]{0,1:T(8,128)S(1)} %get-tuple-element.176, pred[]{:T(512)S(6)} %compare.24, f32[10,1024,2048]{2,1,0:T(8,128)} %get-tuple-element.175, f32[10,2048]{1,0:T(8,128)S(1)} %get-tuple-element.196, ...), kind=kOutput, calls=%fused_computation.8.clone.1 | convolution fusion | flops 5439488000 | bytes 107643392 | tf_op jit(solution)/shard_map/while/body/eval_jaxpr/hqk,khd->qhd/dot_general | solution.py:121
  1042.3 31.8 %bitcast_reduce_fusion.2 = (f32[10,2048]{1,0:T(8,128)S(1)}, f32[10,1024,2048]{2,1,0:T(8,128)}) fusion(bf16[2048,10,128]{2,0,1:T(8,128)(2,1)} %get-tuple-element.200, bf16[8,1024,10,128]{3,1,2,0:T(8,128)(2,1)} %get-tuple-element.199, s32[]{:T(128)} %get-tuple-element.186), kind=kOutput, calls=%fused_computation.1.clone.1 | convolution fusion | flops 5410631680 | bytes 91832832 | tf_op jit(solution)/shard_map/while/body/eval_jaxpr/qhd,khd->hqk/dot_general | solution.py:113
  1074.2 36.5 %bitcast_add_fusion.2 = f32[2048,10,128]{0,2,1:T(8,128)} fusion(f32[2048,10,128]{0,2,1:T(8,128)} %get-tuple-element.189, f32[2048,10]{0,1:T(8,128)S(1)} %get-tuple-element.176, pred[]{:T(512)S(6)} %compare.24, f32[10,1024,2048]{2,1,0:T(8,128)} %get-tuple-element.175, f32[10,2048]{1,0:T(8,128)S(1)} %get-tuple-element.196, ...), kind=kOutput, calls=%fused_computation.8.clone.1 | convolution fusion | flops 5439488000 | bytes 107643392 | tf_op jit(solution)/shard_map/while/body/eval_jaxpr/hqk,khd->qhd/dot_general | solution.py:121
  1137.0 31.8 %bitcast_reduce_fusion.2 = (f32[10,2048]{1,0:T(8,128)S(1)}, f32[10,1024,2048]{2,1,0:T(8,128)}) fusion(bf16[2048,10,128]{2,0,1:T(8,128)(2,1)} %get-tuple-element.200, bf16[8,1024,10,128]{3,1,2,0:T(8,128)(2,1)} %get-tuple-element.199, s32[]{:T(128)} %get-tuple-element.186), kind=kOutput, calls=%fused_computation.1.clone.1 | convolution fusion | flops 5410631680 | bytes 91832832 | tf_op jit(solution)/shard_map/while/body/eval_jaxpr/qhd,khd->hqk/dot_general | solution.py:113
  1168.8 36.5 %bitcast_add_fusion.2 = f32[2048,10,128]{0,2,1:T(8,128)} fusion(f32[2048,10,128]{0,2,1:T(8,128)} %get-tuple-element.189, f32[2048,10]{0,1:T(8,128)S(1)} %get-tuple-element.176, pred[]{:T(512)S(6)} %compare.24, f32[10,1024,2048]{2,1,0:T(8,128)} %get-tuple-element.175, f32[10,2048]{1,0:T(8,128)S(1)} %get-tuple-element.196, ...), kind=kOutput, calls=%fused_computation.8.clone.1 | convolution fusion | flops 5439488000 | bytes 107643392 | tf_op jit(solution)/shard_map/while/body/eval_jaxpr/hqk,khd->qhd/dot_general | solution.py:121
  1231.6 31.8 %bitcast_reduce_fusion.2 = (f32[10,2048]{1,0:T(8,128)S(1)}, f32[10,1024,2048]{2,1,0:T(8,128)}) fusion(bf16[2048,10,128]{2,0,1:T(8,128)(2,1)} %get-tuple-element.200, bf16[8,1024,10,128]{3,1,2,0:T(8,128)(2,1)} %get-tuple-element.199, s32[]{:T(128)} %get-tuple-element.186), kind=kOutput, calls=%fused_computation.1.clone.1 | convolution fusion | flops 5410631680 | bytes 91832832 | tf_op jit(solution)/shard_map/while/body/eval_jaxpr/qhd,khd->hqk/dot_general | solution.py:113
  1263.4 36.5 %bitcast_add_fusion.2 = f32[2048,10,128]{0,2,1:T(8,128)} fusion(f32[2048,10,128]{0,2,1:T(8,128)} %get-tuple-element.189, f32[2048,10]{0,1:T(8,128)S(1)} %get-tuple-element.176, pred[]{:T(512)S(6)} %compare.24, f32[10,1024,2048]{2,1,0:T(8,128)} %get-tuple-element.175, f32[10,2048]{1,0:T(8,128)S(1)} %get-tuple-element.196, ...), kind=kOutput, calls=%fused_computation.8.clone.1 | convolution fusion | flops 5439488000 | bytes 107643392 | tf_op jit(solution)/shard_map/while/body/eval_jaxpr/hqk,khd->qhd/dot_general | solution.py:121
  1326.2 31.8 %bitcast_reduce_fusion.2 = (f32[10,2048]{1,0:T(8,128)S(1)}, f32[10,1024,2048]{2,1,0:T(8,128)}) fusion(bf16[2048,10,128]{2,0,1:T(8,128)(2,1)} %get-tuple-element.200, bf16[8,1024,10,128]{3,1,2,0:T(8,128)(2,1)} %get-tuple-element.199, s32[]{:T(128)} %get-tuple-element.186), kind=kOutput, calls=%fused_computation.1.clone.1 | convolution fusion | flops 5410631680 | bytes 91832832 | tf_op jit(solution)/shard_map/while/body/eval_jaxpr/qhd,khd->hqk/dot_general | solution.py:113
  1358.1 36.5 %bitcast_add_fusion.2 = f32[2048,10,128]{0,2,1:T(8,128)} fusion(f32[2048,10,128]{0,2,1:T(8,128)} %get-tuple-element.189, f32[2048,10]{0,1:T(8,128)S(1)} %get-tuple-element.176, pred[]{:T(512)S(6)} %compare.24, f32[10,1024,2048]{2,1,0:T(8,128)} %get-tuple-element.175, f32[10,2048]{1,0:T(8,128)S(1)} %get-tuple-element.196, ...), kind=kOutput, calls=%fused_computation.8.clone.1 | convolution fusion | flops 5439488000 | bytes 107643392 | tf_op jit(solution)/shard_map/while/body/eval_jaxpr/hqk,khd->qhd/dot_general | solution.py:121
  1463.1 121.3 %all_to_all.46 = bf16[4,512,1280]{2,1,0:T(8,128)(2,1)} all-to-all(bf16[4,512,1280]{2,1,0:T(8,128)(2,1)} %copy.52), channel_id=1, replica_groups=mesh['expert'=2,'seq'=4,'fsdp'=4] {'seq'}, dimensions={0} | all-to-all | bytes 10485760 | tf_op jit(solution)/shard_map/all_to_all | solution.py:163
  (97 shorter events, 521.7 us)
Async XLA Ops:
  6.5 551.7 %all-gather.5.cloned.1.call-start = ((), (), s32[]{:S(2)}) async-start(), calls=%async_computation.4 | async-start | bytes 26214400 | tf_op jit(solution)/shard_map/all_gather | solution.py:156
  11.1 59.5 %collective-permute-start = (bf16[512,1280]{1,0:T(8,128)(2,1)}, bf16[512,1280]{1,0:T(8,128)(2,1)}, u32[]{:S(2)}, u32[]{:S(2)}) collective-permute-start(bf16[512,1280]{1,0:T(8,128)(2,1)} %get-tuple-element.113), channel_id=1, source_target_pairs={{0,4},{4,0},{8,12},{12,8},{1,5},{5,1},{9,13},{13,9},{2,6},{6,2},{1... | collective-permute-start | bytes 3932168 | tf_op jit(solution)/shard_map/ppermute | solution.py:25
  14.1 89.0 %collective-permute-start.1 = (bf16[512,1280]{1,0:T(8,128)(2,1)}, bf16[512,1280]{1,0:T(8,128)(2,1)}, u32[]{:S(2)}, u32[]{:S(2)}) collective-permute-start(bf16[512,1280]{1,0:T(8,128)(2,1)} %get-tuple-element.115), channel_id=1, source_target_pairs={{0,8},{4,12},{8,0},{12,4},{1,9},{5,13},{9,1},{13,5},{2,10},{6,14},... | collective-permute-start | bytes 3932168 | tf_op jit(solution)/shard_map/ppermute | solution.py:25
  16.7 90.5 %collective-permute-start.2 = (bf16[512,1280]{1,0:T(8,128)(2,1)}, bf16[512,1280]{1,0:T(8,128)(2,1)}, u32[]{:S(2)}, u32[]{:S(2)}) collective-permute-start(bf16[512,1280]{1,0:T(8,128)(2,1)} %get-tuple-element.112), channel_id=1, source_target_pairs={{0,12},{4,8},{8,4},{12,0},{1,13},{5,9},{9,5},{13,1},{2,14},{6,10},... | collective-permute-start | bytes 3932168 | tf_op jit(solution)/shard_map/ppermute | solution.py:25
  110.0 3.9 copy-start.1
  110.0 493.5 %all-gather.3.cloned.1.call-start = ((), (), s32[]{:S(2)}) async-start(), calls=%async_computation.3 | async-start | bytes 26214400 | tf_op jit(solution)/shard_map/all_gather | solution.py:155
  147.3 5.2 copy-start.2
  411.0 121.0 %all-to-all-start.1 = ((bf16[512,4,1280]{0,2,1:T(8,128)(2,1)}), bf16[512,4,1280]{0,2,1:T(8,128)(2,1)}, u32[]{:S(2)}, u32[]{:S(2)}) async-start(bf16[512,4,1280]{0,2,1:T(8,128)(2,1)} %convert_element_type.73), calls=%async_computation.1 | async-start | bytes 10485760 | tf_op jit(solution)/shard_map/all_to_all | solution.py:147
  1431.1 13.2 copy-start
Sparse Core Ops, SparseCore 0:
  110.1 153.5 all-gather.4
  389.0 129.8 all-gather.2
